TPU v7x, 32 devices: a whole 2x2x4 slice. The times are simulated.
32 devices in a mesh: region: 2 (over x), shard: 16 (over z, y, core).
Axes of the slice: x: 2, y: 2, z: 4, core: 2. Of those that a mesh axis runs over, the one named last changes fastest.
Arguments:
- queries: bfloat16 [48, 1024], replicated, may hold values from -6 to 6
- database: bfloat16 [16384, 1024], P(('region', 'shard')), may hold values from -6 to 6
- neighbour_ids: int32 [48, 10], replicated, may hold values from 0 to 16383
- tile_weights: bfloat16 [64, 13, 4, 256], P(('region', 'shard')), may hold values from 0.0019989014 to 0.059814453
- tile_columns: int32 [64, 13, 4, 256], P(('region', 'shard')), may hold values from 0 to 255
- tile_owner: int32 [64, 13], P(('region', 'shard')), may hold values from 0 to 15, all different within a row; in each aligned block of 2 rows (0 to 1, 2 to 3, ...) at most 2 rows name the same one
- tile_block: int32 [64, 13], P(('region', 'shard')), may hold values from 0 to 1
Outputs:
- diffused: float32 [48, 16384], P(None, ('region', 'shard'))
Inputs may be any that keep to these rules, and one draw needn't show every extreme that they name: `tile_owner`: each row names 13 different owners; among the rows of one device's blocks no owner is named more than 2 times, and that many in some devices.
All inputs are finite; a program needn't handle non-finite values.
Results may differ from a plain program's by a relative error of at most 0.005.
Values may be sent and summed in bfloat16 or wider, within the bound.
A program may use at most 64 MiB of HBM per device.

v0:
```python
import math

import jax
import jax.numpy as jnp
from jax import lax
from jax.sharding import PartitionSpec as P

EPS = 1e-06
BETA = 0.8


def unit_rows(matrix):
    return matrix / jnp.sqrt(jnp.sum(matrix * matrix, axis=1, keepdims=True) + EPS)


def per_device(
    queries, database, neighbour_ids, tile_weights, tile_columns, tile_owner, tile_block
):
    rows_dev = database.shape[0]
    feature_width = database.shape[1]
    unit_query = unit_rows(queries.astype(jnp.float32)).astype(jnp.bfloat16)
    first_row = lax.axis_index(("region", "shard")) * rows_dev
    similar = lax.dot_general(
        unit_query, database, (((1,), (1,)), ((), ())), preferred_element_type=jnp.float32
    )
    positive = jnp.maximum(similar, 0.0)
    weights = (positive * positive * positive / math.sqrt(feature_width)).astype(jnp.bfloat16)
    local_ids = neighbour_ids - first_row
    row_ids = lax.broadcasted_iota(jnp.int32, (1, 1, rows_dev), 2)
    counts = jnp.sum((local_ids[:, :, None] == row_ids).astype(jnp.float32), axis=1)
    chosen = (counts * weights.astype(jnp.float32)).astype(jnp.bfloat16)
    local_term = jnp.dot(chosen, database, preferred_element_type=jnp.float32)
    expanded_sum = lax.psum(local_term, ("region", "shard")) + unit_query.astype(jnp.float32)
    expanded = unit_rows(expanded_sum).astype(jnp.bfloat16)
    products = lax.dot_general(
        expanded, database, (((1,), (1,)), ((), ())), preferred_element_type=jnp.float32
    )
    scores = jnp.maximum(products, 0.0).astype(jnp.bfloat16)
    blocks_dev = tile_columns.shape[0]
    tile_count = tile_columns.shape[1]
    edge_count = tile_columns.shape[2]
    block_rows = tile_columns.shape[3]
    query_count = scores.shape[0]
    score_blocks = scores.reshape(query_count, blocks_dev, block_rows)
    owners = tile_owner.reshape(-1)
    block_ids = tile_block.reshape(-1)
    sources = owners * blocks_dev + block_ids

    def fetch_blocks(current):
        region_blocks = lax.all_gather(current, "shard", axis=1, tiled=True)
        return region_blocks.reshape(query_count, -1)

    column_base = (sources * block_rows).reshape(blocks_dev, tile_count, 1, 1)
    flat_columns = column_base + tile_columns

    def spread(current):
        flat = fetch_blocks(current)
        total = jnp.zeros((query_count, blocks_dev, block_rows), jnp.float32)
        for edge in range(edge_count):
            reached = jnp.take(flat, flat_columns[:, :, edge, :], axis=1)
            scaled = (
                reached.astype(jnp.float32) * tile_weights[:, :, edge, :].astype(jnp.float32)[None]
            )
            total = total + jnp.sum(scaled, axis=2)
        return total

    source = score_blocks.astype(jnp.float32)
    current = score_blocks
    current = (source + BETA * spread(current)).astype(jnp.bfloat16)
    diffused = source + BETA * spread(current)
    return diffused.reshape(query_count, blocks_dev * block_rows)


def solution(mesh):
    placed = (
        P(),
        P(("region", "shard"), None),
        P(),
        P(("region", "shard"), None, None, None),
        P(("region", "shard"), None, None, None),
        P(("region", "shard"), None),
        P(("region", "shard"), None),
    )
    return jax.shard_map(
        per_device,
        mesh=mesh,
        in_specs=placed,
        out_specs=P(None, ("region", "shard")),
        check_vma=False,
    )
```

profile of v0, /device:TPU:0, one launch (start us, length us, event | category | flops | bytes accessed | tf_op | source)
XLA Modules:
  0.0 358.0 jit_solution(2654204438736871811)
XLA Ops:
  8.6 2.3 fusion.8
  16.4 123.9 %all-reduce.2.cloned.1.call-done = f32[48,1024]{1,0:T(8,128)} async-done(((f32[48,1024]{1,0:T(8,128)}), f32[48,1024]{1,0:T(8,128)}) %all-reduce.2.cloned.1.call-update) | async-done | bytes 196624 | tf_op jit(solution)/shard_map/psum | solution.py:33
  140.3 1.1 multiply_reduce_fusion.8
  141.4 1.4 fusion
  142.8 25.9 %all_gather.6 = bf16[48,32,256]{2,0,1:T(8,128)(2,1)} all-gather(bf16[48,2,256]{2,0,1:T(8,128)(2,1)S(1)} %bitcast.89), channel_id=1, replica_groups=mesh['region'=2,'shard'=16] {'shard'}, dimensions={1}, use_global_device_ids=true | all-gather | bytes 835584 | tf_op jit(solution)/shard_map/all_gather | solution.py:50
  168.7 2.0 copy.158
  170.7 14.2 %gather_fusion = bf16[6656,48]{1,0:T(8,128)(2,1)} fusion(bf16[48,8192]{0,1:T(8,128)(2,1)S(1)} %bitcast.70, s32[7168]{0:T(1024)S(1)} %pad_clamp_fusion.3), kind=kCustom, calls=%fused_computation.clone | custom fusion | bytes 1304576 | tf_op jit(solution)/shard_map/jit(_take)/gather | solution.py:60
  184.9 5.3 %multiply_reduce_fusion.7 = f32[48,2,256]{0,2,1:T(8,128)S(1)} fusion(bf16[2,13,256,48]{3,2,1,0:T(8,128)(2,1)} %bitcast.84, f32[2,13,256]{2,1,0:T(8,128)S(1)} %get-tuple-element.29, pred[2,13,256]{2,1,0:T(8,128)(4,1)S(1)} %copy.154), kind=kLoop, calls=%fused_computation.15 | loop fusion | flops 1253376 | bytes 770560 | tf_op jit(solution)/shard_map/reduce_sum | solution.py:64
  190.3 15.4 %gather_fusion.1 = bf16[6656,48]{1,0:T(8,128)(2,1)} fusion(bf16[48,8192]{0,1:T(8,128)(2,1)S(1)} %bitcast.71, s32[7168]{0:T(1024)} %pad_clamp_fusion.2), kind=kCustom, calls=%fused_computation.1.clone | custom fusion | bytes 1304576 | tf_op jit(solution)/shard_map/jit(_take)/gather | solution.py:60
  205.7 5.4 %multiply_reduce_fusion.6 = f32[48,2,256]{0,2,1:T(8,128)S(1)} fusion(bf16[2,13,256,48]{3,2,1,0:T(8,128)(2,1)} %bitcast.83, f32[2,13,256]{2,1,0:T(8,128)} %get-tuple-element.28, pred[2,13,256]{2,1,0:T(8,128)(4,1)} %copy.164), kind=kLoop, calls=%fused_computation.14 | loop fusion | flops 1253376 | bytes 770560 | tf_op jit(solution)/shard_map/reduce_sum | solution.py:64
  211.9 15.4 %gather_fusion.2 = bf16[6656,48]{1,0:T(8,128)(2,1)} fusion(bf16[48,8192]{0,1:T(8,128)(2,1)S(1)} %bitcast.72, s32[7168]{0:T(1024)} %pad_clamp_fusion.1), kind=kCustom, calls=%fused_computation.2.clone | custom fusion | bytes 1304576 | tf_op jit(solution)/shard_map/jit(_take)/gather | solution.py:60
  227.2 5.4 %multiply_reduce_fusion.5 = f32[48,2,256]{0,2,1:T(8,128)S(1)} fusion(bf16[2,13,256,48]{3,2,1,0:T(8,128)(2,1)} %bitcast.85, f32[2,13,256]{2,1,0:T(8,128)} %get-tuple-element.27, pred[2,13,256]{2,1,0:T(8,128)(4,1)} %copy.172), kind=kLoop, calls=%fused_computation.13 | loop fusion | flops 1253376 | bytes 770560 | tf_op jit(solution)/shard_map/reduce_sum | solution.py:64
  233.4 15.5 %gather_fusion.3 = bf16[6656,48]{1,0:T(8,128)(2,1)} fusion(bf16[48,8192]{0,1:T(8,128)(2,1)S(1)} %bitcast.73, s32[7168]{0:T(1024)} %pad_clamp_fusion), kind=kCustom, calls=%fused_computation.3.clone | custom fusion | bytes 1304576 | tf_op jit(solution)/shard_map/jit(_take)/gather | solution.py:60
  248.9 5.4 %multiply_reduce_fusion.4 = f32[48,2,256]{0,2,1:T(8,128)S(1)} fusion(bf16[2,13,256,48]{3,2,1,0:T(8,128)(2,1)} %bitcast.82, f32[2,13,256]{2,1,0:T(8,128)S(1)} %copy-done.11, pred[2,13,256]{2,1,0:T(8,128)(4,1)S(1)} %copy-done.22), kind=kLoop, calls=%fused_computation.12 | loop fusion | flops 1253376 | bytes 770560 | tf_op jit(solution)/shard_map/reduce_sum | solution.py:64
  254.5 21.0 %all_gather.7 = bf16[48,32,256]{2,0,1:T(8,128)(2,1)} all-gather(bf16[48,2,256]{2,0,1:T(8,128)(2,1)S(1)} %add_convert_fusion), channel_id=1, replica_groups=mesh['region'=2,'shard'=16] {'shard'}, dimensions={1}, use_global_device_ids=true | all-gather | bytes 835584 | tf_op jit(solution)/shard_map/all_gather | solution.py:50
  275.5 2.0 copy.185
  277.5 14.2 %gather_fusion.4 = bf16[6656,48]{1,0:T(8,128)(2,1)} fusion(bf16[48,8192]{0,1:T(8,128)(2,1)S(1)} %bitcast.74, s32[7168]{0:T(1024)S(1)} %copy-done.7), kind=kCustom, calls=%fused_computation.4.clone | custom fusion | bytes 1304576 | tf_op jit(solution)/shard_map/jit(_take)/gather | solution.py:60
  291.6 14.1 %gather_fusion.5 = bf16[6656,48]{1,0:T(8,128)(2,1)} fusion(bf16[48,8192]{0,1:T(8,128)(2,1)S(1)} %bitcast.75, s32[7168]{0:T(1024)S(1)} %copy-done.8), kind=kCustom, calls=%fused_computation.5.clone | custom fusion | bytes 1304576 | tf_op jit(solution)/shard_map/jit(_take)/gather | solution.py:60
  305.8 14.1 %gather_fusion.6 = bf16[6656,48]{1,0:T(8,128)(2,1)} fusion(bf16[48,8192]{0,1:T(8,128)(2,1)S(1)} %bitcast.76, s32[7168]{0:T(1024)S(1)} %copy-done.9), kind=kCustom, calls=%fused_computation.6.clone | custom fusion | bytes 1304576 | tf_op jit(solution)/shard_map/jit(_take)/gather | solution.py:60
  319.9 14.1 %gather_fusion.7 = bf16[6656,48]{1,0:T(8,128)(2,1)} fusion(bf16[48,8192]{0,1:T(8,128)(2,1)S(1)} %bitcast.77, s32[7168]{0:T(1024)S(1)} %copy-done.10), kind=kCustom, calls=%fused_computation.7.clone | custom fusion | bytes 1304576 | tf_op jit(solution)/shard_map/jit(_take)/gather | solution.py:60
  334.1 5.5 %multiply_reduce_fusion.3 = f32[48,2,256]{0,2,1:T(8,128)S(1)} fusion(bf16[2,13,256,48]{3,2,1,0:T(8,128)(2,1)} %bitcast.81, f32[2,13,256]{2,1,0:T(8,128)S(1)} %copy-done.15, pred[2,13,256]{2,1,0:T(8,128)(4,1)S(1)} %copy-done.19), kind=kLoop, calls=%fused_computation.11 | loop fusion | flops 1253376 | bytes 770560 | tf_op jit(solution)/shard_map/reduce_sum | solution.py:64
  339.7 2.4 multiply_reduce_fusion.2
  342.3 5.4 %multiply_reduce_fusion.1 = f32[48,2,256]{0,2,1:T(8,128)S(1)} fusion(bf16[2,13,256,48]{3,2,1,0:T(8,128)(2,1)} %bitcast.79, f32[2,13,256]{2,1,0:T(8,128)S(1)} %copy-done.12, pred[2,13,256]{2,1,0:T(8,128)(4,1)S(1)} %copy-done.21), kind=kLoop, calls=%fused_computation.9 | loop fusion | flops 1253376 | bytes 770560 | tf_op jit(solution)/shard_map/reduce_sum | solution.py:64
  347.9 2.4 multiply_reduce_fusion
  (96 shorter events, 10.3 us)
Async XLA Ops:
  6.5 4.4 %copy-start.25 = (s32[2,13]{1,0:T(2,128)S(1)}, s32[2,13]{1,0:T(2,128)}, u32[]{:S(2)}) copy-start(s32[2,13]{1,0:T(2,128)} %param.14) | copy-start | bytes 316
  6.5 4.4 %copy-start.24 = (s32[2,13]{1,0:T(2,128)S(1)}, s32[2,13]{1,0:T(2,128)}, u32[]{:S(2)}) copy-start(s32[2,13]{1,0:T(2,128)} %param.15) | copy-start | bytes 316
  6.5 4.4 %copy-start.17 = (s32[2,13,4,256]{3,2,1,0:T(4,128)S(1)}, s32[2,13,4,256]{3,2,1,0:T(4,128)}, u32[]{:S(2)}) copy-start(s32[2,13,4,256]{3,2,1,0:T(4,128)} %param.13) | copy-start | bytes 319492
  6.5 133.7 %all-reduce.2.cloned.1.call-start = ((), (), s32[]{:S(2)}) async-start(), calls=%async_computation | async-start | bytes 393216 | tf_op jit(solution)/shard_map/psum | solution.py:33
  10.9 129.4 %copy-start.3 = (bf16[48,1024]{1,0:T(8,128)(2,1)S(1)}, bf16[48,1024]{1,0:T(8,128)(2,1)}, u32[]{:S(2)}) copy-start(bf16[48,1024]{1,0:T(8,128)(2,1)} %param.9) | copy-start | bytes 294916
  11.3 159.5 %copy-start.6 = (s32[7168]{0:T(1024)}, s32[7168]{0:T(1024)S(1)}, u32[]{:S(2)}) copy-start(s32[7168]{0:T(1024)S(1)} %pad_clamp_fusion.3) | copy-start | bytes 86020
  11.3 173.6 %copy-start.18 = (pred[2,13,256]{2,1,0:T(8,128)(4,1)}, pred[2,13,256]{2,1,0:T(8,128)(4,1)S(1)}, u32[]{:S(2)}) copy-start(pred[2,13,256]{2,1,0:T(8,128)(4,1)S(1)} %copy.154) | copy-start | bytes 19972
  15.2 169.7 %copy-start.14 = (f32[2,13,256]{2,1,0:T(8,128)}, f32[2,13,256]{2,1,0:T(8,128)S(1)}, u32[]{:S(2)}) copy-start(f32[2,13,256]{2,1,0:T(8,128)S(1)} %get-tuple-element.29) | copy-start | bytes 79876
  233.4 15.5 %copy-start.11 = (f32[2,13,256]{2,1,0:T(8,128)S(1)}, f32[2,13,256]{2,1,0:T(8,128)}, u32[]{:S(2)}) copy-start(f32[2,13,256]{2,1,0:T(8,128)} %get-tuple-element.26) | copy-start | bytes 79876
  233.4 15.5 %copy-start.22 = (pred[2,13,256]{2,1,0:T(8,128)(4,1)S(1)}, pred[2,13,256]{2,1,0:T(8,128)(4,1)}, u32[]{:S(2)}) copy-start(pred[2,13,256]{2,1,0:T(8,128)(4,1)} %copy.179) | copy-start | bytes 19972
  248.9 5.5 %copy-start.4 = (f32[48,2,256]{2,0,1:T(8,128)S(1)}, f32[48,2,256]{2,0,1:T(8,128)}, u32[]{:S(2)}) copy-start(f32[48,2,256]{2,0,1:T(8,128)} %copy.170) | copy-start | bytes 294916
  248.9 5.5 %copy-start.5 = (f32[48,2,256]{2,0,1:T(8,128)S(1)}, f32[48,2,256]{2,0,1:T(8,128)}, u32[]{:S(2)}) copy-start(f32[48,2,256]{2,0,1:T(8,128)} %copy.177) | copy-start | bytes 294916
  254.4 23.0 %copy-start.7 = (s32[7168]{0:T(1024)S(1)}, s32[7168]{0:T(1024)}, u32[]{:S(2)}) copy-start(s32[7168]{0:T(1024)} %copy-done.6) | copy-start | bytes 86020
  277.5 14.2 %copy-start.8 = (s32[7168]{0:T(1024)S(1)}, s32[7168]{0:T(1024)}, u32[]{:S(2)}) copy-start(s32[7168]{0:T(1024)} %pad_clamp_fusion.2) | copy-start | bytes 86020
  291.6 14.1 %copy-start.9 = (s32[7168]{0:T(1024)S(1)}, s32[7168]{0:T(1024)}, u32[]{:S(2)}) copy-start(s32[7168]{0:T(1024)} %pad_clamp_fusion.1) | copy-start | bytes 86020
  305.8 14.2 %copy-start.10 = (s32[7168]{0:T(1024)S(1)}, s32[7168]{0:T(1024)}, u32[]{:S(2)}) copy-start(s32[7168]{0:T(1024)} %pad_clamp_fusion) | copy-start | bytes 86020
  319.9 14.2 %copy-start.15 = (f32[2,13,256]{2,1,0:T(8,128)S(1)}, f32[2,13,256]{2,1,0:T(8,128)}, u32[]{:S(2)}) copy-start(f32[2,13,256]{2,1,0:T(8,128)} %copy-done.14) | copy-start | bytes 79876
  319.9 14.2 %copy-start.19 = (pred[2,13,256]{2,1,0:T(8,128)(4,1)S(1)}, pred[2,13,256]{2,1,0:T(8,128)(4,1)}, u32[]{:S(2)}) copy-start(pred[2,13,256]{2,1,0:T(8,128)(4,1)} %copy-done.18) | copy-start | bytes 19972
  334.1 5.6 %copy-start.2 = (bf16[6656,48]{1,0:T(8,128)(2,1)S(1)}, bf16[6656,48]{1,0:T(8,128)(2,1)}, u32[]{:S(2)}) copy-start(bf16[6656,48]{1,0:T(8,128)(2,1)} %gather_fusion.5) | copy-start | bytes 1916932
  334.1 5.6 %copy-start.13 = (f32[2,13,256]{2,1,0:T(8,128)S(1)}, f32[2,13,256]{2,1,0:T(8,128)}, u32[]{:S(2)}) copy-start(f32[2,13,256]{2,1,0:T(8,128)} %get-tuple-element.28) | copy-start | bytes 79876
  334.1 5.6 %copy-start.20 = (pred[2,13,256]{2,1,0:T(8,128)(4,1)S(1)}, pred[2,13,256]{2,1,0:T(8,128)(4,1)}, u32[]{:S(2)}) copy-start(pred[2,13,256]{2,1,0:T(8,128)(4,1)} %copy.164) | copy-start | bytes 19972
  339.6 2.7 copy-start.12
  342.1 5.7 %copy-start.1 = (bf16[6656,48]{1,0:T(8,128)(2,1)S(1)}, bf16[6656,48]{1,0:T(8,128)(2,1)}, u32[]{:S(2)}) copy-start(bf16[6656,48]{1,0:T(8,128)(2,1)} %gather_fusion.7) | copy-start | bytes 1916932
  342.2 5.7 %copy-start.23 = (pred[2,13,256]{2,1,0:T(8,128)(4,1)S(1)}, pred[2,13,256]{2,1,0:T(8,128)(4,1)}, u32[]{:S(2)}) copy-start(pred[2,13,256]{2,1,0:T(8,128)(4,1)} %copy.179) | copy-start | bytes 19972
  (3 other events, 7.5 us)
Sparse Core Ops, SparseCore 0:
  12.9 127.3 all-reduce.1
where the time goes:
time: 360 us; the launch traced here: 358 us
  local copies, waits for them, and re-layouts  125 us (35%)
  waiting for transfers between devices  124 us (34%)
  blocking collectives  46.9 us (13%)
  other arithmetic  44.3 us (12%)
  between operations  13.9 us (4%)
  matrix products  3.67 us (1%)
    psum x1, waiting for transfers between devices, per_device(): lax.psum(local_term, ('region', 'shard')) + unit_query.astype(jnp.float32)  124 us
    gather x8, local copies, waits for them, and re-layouts, spread(): reached = jnp.take(flat, flat_columns[:, :, edge, :], axis=1)  117 us
    all_gather x2, blocking collectives, fetch_blocks(): region_blocks = lax.all_gather(current, 'shard', axis=1, tiled=True)  46.9 us
    reduce_sum x8, other arithmetic, spread(): total = total + jnp.sum(scaled, axis=2)  37.2 us
  transfers between devices with their start and end apart: 1, of which 1 were waited for; matrix products, arithmetic and copies ran while one was open for 1% of the time, Pallas kernels for 0%

commit v1 on v0

v1 whole, which is shorter than its diff:
```python
import functools
import math

import jax
import jax.numpy as jnp
from jax import lax
from jax.experimental import pallas as pl
from jax.experimental.pallas import tpu as pltpu
from jax.sharding import PartitionSpec as P

EPS = 1e-06
BETA = 0.8
LANES = 128
F32 = jnp.float32
BF16 = jnp.bfloat16


def flip(index, mask):
    bit = 1
    while bit <= mask:
        if mask & bit:
            index = index + bit - 2 * bit * ((index // bit) % 2)
        bit *= 2
    return index


class Plan:
    def __init__(self, regions, shards, width):
        self.regions, self.shards = regions, shards
        self.slices = width // LANES
        self.inner = self.slices // regions
        self.outer = shards // self.inner
        assert self.inner * regions * LANES == width and self.outer * self.inner == shards
        assert self.inner == 1 or self.inner % 2 == 0
        if self.inner > 2:
            self.mid = self.inner // 2
        else:
            self.mid = 1 << (((shards // 2).bit_length() - 1) // 2)
        self.far = shards // (2 * self.mid)
        assert self.far * self.mid * 2 == shards


def kernel(
    plan,
    q_ref,
    db_hbm,
    ids_ref,
    w_ref,
    col_ref,
    owner_ref,
    block_ref,
    out_ref,
    db,
    uq,
    part,
    rs_buf,
    z_send,
    z_buf,
    full,
    tiles,
    scores_ref,
    all1,
    all2,
    load_sem,
    rs_sems,
    z_sems,
    ag_sems,
    far_sems,
    mid_sems,
    core_sems,
):
    rows_dev, width = db.shape
    blocks_dev, tile_count, edge_count, block_rows = w_ref.shape
    slices, inner, outer = plan.slices, plan.inner, plan.outer
    region, shard = lax.axis_index("region"), lax.axis_index("shard")
    group_at, group = shard % inner, shard // inner
    slot = region * inner + group_at

    def member(index):
        return (index // inner, group * inner + index % inner)

    def across(index):
        return (region, index * inner + group_at)

    load = pltpu.make_async_copy(db_hbm, db, load_sem)
    load.start()
    barrier = pltpu.get_barrier_semaphore()
    for d in range(1, slices):
        pl.semaphore_signal(
            barrier, inc=1, device_id=member(flip(slot, d)), device_id_type=pl.DeviceIdType.MESH
        )
    for d in range(1, outer):
        pl.semaphore_signal(
            barrier, inc=1, device_id=across(flip(group, d)), device_id_type=pl.DeviceIdType.MESH
        )

    def send(src, dst, sems, at, device):
        copy = pltpu.make_async_remote_copy(
            src_ref=src,
            dst_ref=dst,
            send_sem=sems.at[(0,) + at],
            recv_sem=sems.at[(1,) + at],
            device_id=device,
            device_id_type=pl.DeviceIdType.MESH,
        )
        copy.start()
        return copy

    row_of = lax.broadcasted_iota(jnp.int32, (block_rows, block_rows), 0).astype(F32).astype(BF16)

    def build(t, carry):
        b, j = t // tile_count, t % tile_count
        columns = col_ref[b, j].astype(F32).astype(BF16)
        weights = w_ref[b, j]
        acc = None
        for e in range(edge_count):
            hit = row_of == columns[e : e + 1, :]
            term = jnp.where(hit, weights[e : e + 1, :], jnp.zeros((), BF16))
            acc = term if acc is None else acc + term
        tiles[t] = acc
        return carry

    total_tiles = blocks_dev * tile_count
    cuts = [0, total_tiles * 3 // 10, total_tiles * 7 // 10, total_tiles]

    q = q_ref[...].astype(F32)
    unit = (q / jnp.sqrt(jnp.sum(q * q, axis=1, keepdims=True) + EPS)).astype(BF16)
    for p in range(slices):
        uq[p] = unit[:, p * LANES : (p + 1) * LANES].astype(F32)
    ids = ids_ref[...] - (region * plan.shards + shard) * rows_dev
    row_ids = lax.broadcasted_iota(jnp.int32, (ids.shape[0], rows_dev), 1)
    counts = jnp.zeros((ids.shape[0], rows_dev), F32)
    for k in range(ids.shape[1]):
        counts = counts + jnp.where(ids[:, k : k + 1] == row_ids, 1.0, 0.0)
    load.wait()
    data = db[...]
    similar = lax.dot_general(unit, data, (((1,), (1,)), ((), ())), preferred_element_type=F32)
    positive = jnp.maximum(similar, 0.0)
    weights = (positive * positive * positive / math.sqrt(width)).astype(BF16)
    chosen = (counts * weights.astype(F32)).astype(BF16)
    local = jnp.dot(chosen, data, preferred_element_type=F32)
    for p in range(slices):
        part[p] = local[:, p * LANES : (p + 1) * LANES].astype(BF16)

    pl.semaphore_wait(barrier, slices - 1 + outer - 1)

    copies = []
    for d in range(1, slices):
        peer = flip(slot, d)
        copies.append(send(part.at[peer], rs_buf.at[d], rs_sems, (d,), member(peer)))
    lax.fori_loop(cuts[0], cuts[1], build, 0)
    total = part[slot].astype(F32)
    for d in range(1, slices):
        copies[d - 1].wait_recv()
        total = total + rs_buf[d].astype(F32)
    z_send[...] = total.astype(BF16)
    pending = copies

    copies = []
    for d in range(1, outer):
        copies.append(send(z_send, z_buf.at[d], z_sems, (d,), across(flip(group, d))))
    lax.fori_loop(cuts[1], cuts[2], build, 0)
    total = total + uq[slot]
    for d in range(1, outer):
        copies[d - 1].wait_recv()
        total = total + z_buf[d].astype(F32)
    full[slot] = total.astype(BF16)
    pending = pending + copies

    copies = []
    for d in range(1, slices):
        copies.append(
            send(full.at[slot], full.at[slot], ag_sems, (d,), member(flip(slot, d)))
        )
    lax.fori_loop(cuts[2], cuts[3], build, 0)
    for copy in copies:
        copy.wait_recv()
    pending = pending + copies

    expanded = jnp.concatenate([full[p] for p in range(slices)], axis=1)
    wide = expanded.astype(F32)
    scale = 1.0 / jnp.sqrt(jnp.sum(wide * wide, axis=1, keepdims=True) + EPS)
    products = lax.dot_general(
        expanded, data, (((1,), (1,)), ((), ())), preferred_element_type=F32
    )
    scores = jnp.maximum(products * scale, 0.0).astype(BF16)

    mid, far = plan.mid, plan.far
    far_at, mid_at, core_at = shard // (2 * mid), (shard // 2) % mid, shard % 2

    def share(buf, which):
        def place(f, m, c):
            return (f * mid + m) * 2 + c

        done = []

        def push(f, m, sems, at, device):
            source = buf.at[place(f, m, core_at)]
            done.append(send(source, source, sems, (which,) + at, (region, device)))
            return done[-1]

        partner = place(far_at, mid_at, 1 - core_at)

        def to_mids(fd, f):
            return [
                push(f, mid_at, mid_sems, (md, fd), place(far_at, flip(mid_at, md), core_at))
                for md in range(1, mid)
            ]

        core_copies, mid_copies = [], []
        far_copies = [
            push(far_at, mid_at, far_sems, (fd,), place(flip(far_at, fd), mid_at, core_at))
            for fd in range(far - 1, 0, -1)
        ][::-1]
        mid_copies.append(to_mids(0, far_at))
        core_copies.append(push(far_at, mid_at, core_sems, (0, 0), partner))

        def mids_arrive(fd):
            for md in range(1, mid):
                mid_copies[fd][md - 1].wait_recv()
                core_copies.append(
                    push(flip(far_at, fd), flip(mid_at, md), core_sems, (md, fd), partner)
                )

        for fd in range(1, far):
            far_copies[fd - 1].wait_recv()
            mid_copies.append(to_mids(fd, flip(far_at, fd)))
            core_copies.append(push(flip(far_at, fd), mid_at, core_sems, (0, fd), partner))
            mids_arrive(fd - 1)
        mids_arrive(far - 1)
        for copy in core_copies:
            copy.wait_recv()
        return done

    def spread(buf):
        sums = []
        for b in range(blocks_dev):
            acc = None
            for j in range(tile_count):
                values = buf[owner_ref[b, j], block_ref[b, j]]
                term = jnp.dot(
                    values, tiles[b * tile_count + j], preferred_element_type=F32
                )
                acc = term if acc is None else acc + term
            sums.append(acc)
        return sums

    for b in range(blocks_dev):
        own = scores[:, b * block_rows : (b + 1) * block_rows]
        scores_ref[b] = own.astype(F32)
        all1[shard, b] = own
    pending = pending + share(all1, 0)
    sums = spread(all1)
    for b in range(blocks_dev):
        all2[shard, b] = (scores_ref[b] + BETA * sums[b]).astype(BF16)
    pending = pending + share(all2, 1)
    sums = spread(all2)
    for b in range(blocks_dev):
        out_ref[:, b * block_rows : (b + 1) * block_rows] = scores_ref[b] + BETA * sums[b]
    for copy in pending:
        copy.wait_send()


def per_device(
    plan, queries, database, neighbour_ids, tile_weights, tile_columns, tile_owner, tile_block
):
    query_count, width = queries.shape
    rows_dev = database.shape[0]
    blocks_dev, tile_count, edge_count, block_rows = tile_weights.shape
    vmem = pl.BlockSpec(memory_space=pltpu.VMEM)
    smem = pl.BlockSpec(memory_space=pltpu.SMEM)
    dma = pltpu.SemaphoreType.DMA
    state = (plan.shards, blocks_dev, query_count, block_rows)
    piece = (query_count, LANES)
    return pl.pallas_call(
        functools.partial(kernel, plan),
        out_shape=jax.ShapeDtypeStruct((query_count, rows_dev), F32),
        in_specs=[vmem, pl.BlockSpec(memory_space=pl.ANY), vmem, vmem, vmem, smem, smem],
        out_specs=vmem,
        scratch_shapes=[
            pltpu.VMEM((rows_dev, width), BF16),
            pltpu.VMEM((plan.slices,) + piece, F32),
            pltpu.VMEM((plan.slices,) + piece, BF16),
            pltpu.VMEM((plan.slices,) + piece, BF16),
            pltpu.VMEM(piece, BF16),
            pltpu.VMEM((plan.outer,) + piece, BF16),
            pltpu.VMEM((plan.slices,) + piece, BF16),
            pltpu.VMEM((blocks_dev * tile_count, block_rows, block_rows), BF16),
            pltpu.VMEM((blocks_dev, query_count, block_rows), F32),
            pltpu.VMEM(state, BF16),
            pltpu.VMEM(state, BF16),
            dma,
            dma((2, plan.slices)),
            dma((2, plan.outer)),
            dma((2, plan.slices)),
            dma((2, 2, plan.far)),
            dma((2, 2, plan.mid, plan.far)),
            dma((2, 2, plan.mid, plan.far)),
        ],
        compiler_params=pltpu.CompilerParams(collective_id=0, has_side_effects=True),
        name="expand_and_diffuse",
    )(queries, database, neighbour_ids, tile_weights, tile_columns, tile_owner, tile_block)


def solution(mesh):
    plan_of = functools.partial(Plan, mesh.shape["region"], mesh.shape["shard"])

    def body(queries, *rest):
        return per_device(plan_of(queries.shape[1]), queries, *rest)

    placed = (
        P(),
        P(("region", "shard"), None),
        P(),
        P(("region", "shard"), None, None, None),
        P(("region", "shard"), None, None, None),
        P(("region", "shard"), None),
        P(("region", "shard"), None),
    )
    return jax.shard_map(
        body,
        mesh=mesh,
        in_specs=placed,
        out_specs=P(None, ("region", "shard")),
        check_vma=False,
    )
```

time: 360 us -> 46.2 us (0.13)
  waiting for transfers between devices: 124 us -> 0 us
  local copies, waits for them, and re-layouts: 125 us -> 2.93 us
  blocking collectives: 46.9 us -> 0 us
  other arithmetic: 44.3 us -> 0 us
  Pallas kernels: 0 us -> 42.6 us
  between operations: 13.9 us -> 0.01 us
  matrix products: 3.67 us -> 0 us
    psum x1 -> x0, waiting for transfers between devices: 124 us -> none  [per_device(): lax.psum(local_term, ('region', 'shard')) + unit_query.astype(jnp.float32)]
    gather x8 -> x0, local copies, waits for them, and re-layouts: 117 us -> none  [spread(): reached = jnp.take(flat, flat_columns[:, :, edge, :], axis=1)]
    all_gather x2 -> x0, blocking collectives: 46.9 us -> none  [fetch_blocks(): region_blocks = lax.all_gather(current, 'shard', axis=1, tiled=True)]
    pallas_call x0 -> x1, Pallas kernels: none -> 42.6 us  [per_device(): pl.pallas_call(functools.partial(kernel, plan), out_shape=jax.ShapeDtypeS...]
    reduce_sum x11 -> x0, other arithmetic: 39.5 us -> none  [the longest x8 37.2 us: spread(): total = total + jnp.sum(scaled, axis=2)]
    all_gather x2 -> x0, local copies, waits for them, and re-layouts: 3.95 us -> none  [fetch_blocks(): region_blocks = lax.all_gather(current, 'shard', axis=1, tiled=True)]
    dot_general x2 -> x0, matrix products: 3.67 us -> none  [the longest x1 2.29 us: per_device(): local_term = jnp.dot(chosen, database, preferred_element_type=jnp.float32)]
  transfers between devices with their start and end apart: 1 -> 0, of which waited for: 1 -> 0; matrix products, arithmetic and copies ran while one was open for 1% -> 0% of each run, Pallas kernels for 0% -> 0%
where the time goes in v1:
time: 46.2 us; the launch traced here: 45.5 us
  Pallas kernels  42.6 us (92%)
  local copies, waits for them, and re-layouts  2.93 us (6%)
    pallas_call x1, Pallas kernels, per_device(): pl.pallas_call(functools.partial(kernel, plan), out_shape=jax.ShapeDtypeS...  42.6 us
    unnamed x2, local copies, waits for them, and re-layouts  2.93 us

profile of v1, /device:TPU:0, one launch (start us, length us, event | category | flops | bytes accessed | tf_op | source)
XLA Modules:
  0.0 45.5 jit_solution(11686587100883565681)
XLA Ops:
  0.0 1.4 %copy.8.ids_ref = s32[48,10]{1,0:T(8,128)} copy(s32[48,10]{0,1:T(8,128)} %param.9) | data formatting | bytes 3840 | tf_op args[2]
  1.4 42.6 %expand_and_diffuse.1 = f32[48,512]{1,0:T(8,128)} custom-call(bf16[48,1024]{1,0:T(8,128)(2,1)} %q_ref.1, bf16[512,1024]{1,0:T(8,128)(2,1)} %db_hbm.1, s32[48,10]{1,0:T(8,128)} %copy.8.ids_ref, bf16[2,13,4,256]{3,2,1,0:T(4,128)(2,1)} %w_ref.1, s32[2,13,4,256]{3,2,1,0:T(4,128)} %col_ref.1, s32[2,13]{1,0:T(2,128)} %owner_ref.1, s32[2,13]{1,0:T(2,128)} %block_ref.1), custom_call_target="tpu_custom_call" | custom-call | tf_op jit(solution)/shard_map/expand_and_diffuse/pallas_call | solution.py:275
  44.0 1.5 %copy.10 = f32[48,512]{1,0:T(8,128)} copy(f32[48,512]{1,0:T(8,128)} %expand_and_diffuse.1) | data formatting | bytes 196608

commit v2 on v1

--- a/solution.py
+++ b/solution.py
@@ -9,7 +9,9 @@
 from jax.sharding import PartitionSpec as P
 
 EPS = 1e-06
+LAG = 2
 BETA = 0.8
+CUTS = (0, 5, 12, 17, 26)
 LANES = 128
 F32 = jnp.float32
 BF16 = jnp.bfloat16
@@ -45,12 +47,14 @@
     q_ref,
     db_hbm,
     ids_ref,
-    w_ref,
-    col_ref,
+    w_hbm,
+    col_hbm,
     owner_ref,
     block_ref,
     out_ref,
     db,
+    w_ref,
+    col_ref,
     uq,
     part,
     rs_buf,
@@ -82,8 +86,14 @@
     def across(index):
         return (region, index * inner + group_at)
 
-    load = pltpu.make_async_copy(db_hbm, db, load_sem)
+    load = pltpu.make_async_copy(db_hbm, db, load_sem.at[0])
     load.start()
+    tile_loads = [
+        pltpu.make_async_copy(w_hbm, w_ref, load_sem.at[1]),
+        pltpu.make_async_copy(col_hbm, col_ref, load_sem.at[2]),
+    ]
+    for tile_load in tile_loads:
+        tile_load.start()
     barrier = pltpu.get_barrier_semaphore()
     for d in range(1, slices):
         pl.semaphore_signal(
@@ -121,13 +131,13 @@
         return carry
 
     total_tiles = blocks_dev * tile_count
-    cuts = [0, total_tiles * 3 // 10, total_tiles * 7 // 10, total_tiles]
+    cuts = [total_tiles * part_of // 26 for part_of in CUTS]
 
     q = q_ref[...].astype(F32)
     unit = (q / jnp.sqrt(jnp.sum(q * q, axis=1, keepdims=True) + EPS)).astype(BF16)
     for p in range(slices):
         uq[p] = unit[:, p * LANES : (p + 1) * LANES].astype(F32)
-    ids = ids_ref[...] - (region * plan.shards + shard) * rows_dev
+    ids = ids_ref[...].T - (region * plan.shards + shard) * rows_dev
     row_ids = lax.broadcasted_iota(jnp.int32, (ids.shape[0], rows_dev), 1)
     counts = jnp.zeros((ids.shape[0], rows_dev), F32)
     for k in range(ids.shape[1]):
@@ -142,6 +152,8 @@
     for p in range(slices):
         part[p] = local[:, p * LANES : (p + 1) * LANES].astype(BF16)
 
+    for tile_load in tile_loads:
+        tile_load.wait()
     pl.semaphore_wait(barrier, slices - 1 + outer - 1)
 
     copies = []
@@ -188,46 +200,62 @@
     mid, far = plan.mid, plan.far
     far_at, mid_at, core_at = shard // (2 * mid), (shard // 2) % mid, shard % 2
 
-    def share(buf, which):
+    def share(buf, which, meanwhile=None):
         def place(f, m, c):
             return (f * mid + m) * 2 + c
 
         done = []
 
-        def push(f, m, sems, at, device):
-            source = buf.at[place(f, m, core_at)]
-            done.append(send(source, source, sems, (which,) + at, (region, device)))
-            return done[-1]
+        def push(f, m, piece, sems, at, device):
+            source = buf.at[place(f, m, core_at), piece]
+            copy = send(source, source, sems, (which, piece) + at, (region, device))
+            done.append(copy)
+            return copy
 
         partner = place(far_at, mid_at, 1 - core_at)
-
-        def to_mids(fd, f):
+        core_copies = []
+
+        def to_mids(fd, piece):
+            f = flip(far_at, fd)
             return [
-                push(f, mid_at, mid_sems, (md, fd), place(far_at, flip(mid_at, md), core_at))
+                push(f, mid_at, piece, mid_sems, (md, fd), place(far_at, flip(mid_at, md), core_at))
                 for md in range(1, mid)
             ]
 
-        core_copies, mid_copies = [], []
-        far_copies = [
-            push(far_at, mid_at, far_sems, (fd,), place(flip(far_at, fd), mid_at, core_at))
-            for fd in range(far - 1, 0, -1)
-        ][::-1]
-        mid_copies.append(to_mids(0, far_at))
-        core_copies.append(push(far_at, mid_at, core_sems, (0, 0), partner))
-
-        def mids_arrive(fd):
+        def to_core(md, fd, piece):
+            f, m = flip(far_at, fd), flip(mid_at, md)
+            core_copies.append(push(f, m, piece, core_sems, (md, fd), partner))
+
+        order = [1] + list(range(far - 1, 1, -1)) if far > 1 else []
+        steps = [(fd, piece) for fd in order for piece in range(blocks_dev)]
+        far_copies = {
+            (fd, piece): push(
+                far_at, mid_at, piece, far_sems, (fd,), place(flip(far_at, fd), mid_at, core_at)
+            )
+            for fd, piece in steps
+        }
+        queue = []
+        for piece in range(blocks_dev):
+            queue.append((0, piece, to_mids(0, piece)))
+        for piece in range(blocks_dev):
+            to_core(0, 0, piece)
+        if meanwhile is not None:
+            meanwhile()
+
+        def mids_arrive():
+            fd, piece, copies = queue.pop(0)
             for md in range(1, mid):
-                mid_copies[fd][md - 1].wait_recv()
-                core_copies.append(
-                    push(flip(far_at, fd), flip(mid_at, md), core_sems, (md, fd), partner)
-                )
-
-        for fd in range(1, far):
-            far_copies[fd - 1].wait_recv()
-            mid_copies.append(to_mids(fd, flip(far_at, fd)))
-            core_copies.append(push(flip(far_at, fd), mid_at, core_sems, (0, fd), partner))
-            mids_arrive(fd - 1)
-        mids_arrive(far - 1)
+                copies[md - 1].wait_recv()
+                to_core(md, fd, piece)
+
+        for at, (fd, piece) in enumerate(steps):
+            far_copies[fd, piece].wait_recv()
+            queue.append((fd, piece, to_mids(fd, piece)))
+            to_core(0, fd, piece)
+            if at >= LAG:
+                mids_arrive()
+        while queue:
+            mids_arrive()
         for copy in core_copies:
             copy.wait_recv()
         return done
@@ -249,7 +277,7 @@
         own = scores[:, b * block_rows : (b + 1) * block_rows]
         scores_ref[b] = own.astype(F32)
         all1[shard, b] = own
-    pending = pending + share(all1, 0)
+    pending = pending + share(all1, 0, lambda: lax.fori_loop(cuts[3], cuts[4], build, 0))
     sums = spread(all1)
     for b in range(blocks_dev):
         all2[shard, b] = (scores_ref[b] + BETA * sums[b]).astype(BF16)
@@ -269,16 +297,19 @@
     blocks_dev, tile_count, edge_count, block_rows = tile_weights.shape
     vmem = pl.BlockSpec(memory_space=pltpu.VMEM)
     smem = pl.BlockSpec(memory_space=pltpu.SMEM)
+    anywhere = pl.BlockSpec(memory_space=pl.ANY)
     dma = pltpu.SemaphoreType.DMA
     state = (plan.shards, blocks_dev, query_count, block_rows)
     piece = (query_count, LANES)
     return pl.pallas_call(
         functools.partial(kernel, plan),
         out_shape=jax.ShapeDtypeStruct((query_count, rows_dev), F32),
-        in_specs=[vmem, pl.BlockSpec(memory_space=pl.ANY), vmem, vmem, vmem, smem, smem],
+        in_specs=[vmem, anywhere, vmem, anywhere, anywhere, smem, smem],
         out_specs=vmem,
         scratch_shapes=[
             pltpu.VMEM((rows_dev, width), BF16),
+            pltpu.VMEM(tile_weights.shape, BF16),
+            pltpu.VMEM(tile_columns.shape, jnp.int32),
             pltpu.VMEM((plan.slices,) + piece, F32),
             pltpu.VMEM((plan.slices,) + piece, BF16),
             pltpu.VMEM((plan.slices,) + piece, BF16),
@@ -289,17 +320,17 @@
             pltpu.VMEM((blocks_dev, query_count, block_rows), F32),
             pltpu.VMEM(state, BF16),
             pltpu.VMEM(state, BF16),
-            dma,
+            dma((3,)),
             dma((2, plan.slices)),
             dma((2, plan.outer)),
             dma((2, plan.slices)),
-            dma((2, 2, plan.far)),
-            dma((2, 2, plan.mid, plan.far)),
-            dma((2, 2, plan.mid, plan.far)),
+            dma((2, 2, blocks_dev, plan.far)),
+            dma((2, 2, blocks_dev, plan.mid, plan.far)),
+            dma((2, 2, blocks_dev, plan.mid, plan.far)),
         ],
         compiler_params=pltpu.CompilerParams(collective_id=0, has_side_effects=True),
         name="expand_and_diffuse",
-    )(queries, database, neighbour_ids, tile_weights, tile_columns, tile_owner, tile_block)
+    )(queries, database, neighbour_ids.T, tile_weights, tile_columns, tile_owner, tile_block)
 
 
 def solution(mesh):

time: 46.2 us -> 42.2 us (0.913); the launches traced: 45.5 us -> 42 us
  Pallas kernels: 42.6 us -> 40.5 us
  local copies, waits for them, and re-layouts: 2.93 us -> 1.54 us
    pallas_call x1, Pallas kernels: 42.6 us -> 40.5 us  [per_device(): pl.pallas_call(functools.partial(kernel, plan), out_shape=jax.ShapeDtypeS...]
    unnamed x2 -> x1, local copies, waits for them, and re-layouts: 2.93 us -> 1.54 us
where the time goes in v2:
time: 42.2 us; the launch traced here: 42 us
  Pallas kernels  40.5 us (96%)
  local copies, waits for them, and re-layouts  1.54 us (4%)
    pallas_call x1, Pallas kernels, per_device(): pl.pallas_call(functools.partial(kernel, plan), out_shape=jax.ShapeDtypeS...  40.5 us
    unnamed x1, local copies, waits for them, and re-layouts  1.54 us

profile of v2, /device:TPU:0, one launch (start us, length us, event | category | flops | bytes accessed | tf_op | source)
XLA Modules:
  0.0 42.0 jit_solution(14887108898701613313)
XLA Ops:
  0.0 40.5 %expand_and_diffuse.1 = f32[48,512]{1,0:T(8,128)} custom-call(bf16[48,1024]{1,0:T(8,128)(2,1)} %q_ref.1, bf16[512,1024]{1,0:T(8,128)(2,1)} %db_hbm.1, s32[10,48]{1,0:T(8,128)} %bitcast.1, bf16[2,13,4,256]{3,2,1,0:T(4,128)(2,1)} %w_hbm.1, s32[2,13,4,256]{3,2,1,0:T(4,128)} %col_hbm.1, s32[2,13]{1,0:T(2,128)} %owner_ref.1, s32[2,13]{1,0:T(2,128)} %block_ref.1), custom_call_target="tpu_custom_call" | custom-call | tf_op jit(solution)/shard_map/expand_and_diffuse/pallas_call | solution.py:304
  40.5 1.5 %copy.9 = f32[48,512]{1,0:T(8,128)} copy(f32[48,512]{1,0:T(8,128)} %expand_and_diffuse.1) | data formatting | bytes 196608

commit v3 on v2

--- a/solution.py
+++ b/solution.py
@@ -9,9 +9,9 @@
 from jax.sharding import PartitionSpec as P
 
 EPS = 1e-06
-LAG = 2
+LAG = 1
 BETA = 0.8
-CUTS = (0, 5, 12, 17, 26)
+CUTS = (0, 0, 8, 16, 26)
 LANES = 128
 F32 = jnp.float32
 BF16 = jnp.bfloat16
@@ -49,12 +49,14 @@
     ids_ref,
     w_hbm,
     col_hbm,
-    owner_ref,
-    block_ref,
+    owner_hbm,
+    block_hbm,
     out_ref,
     db,
     w_ref,
     col_ref,
+    owner_ref,
+    block_ref,
     uq,
     part,
     rs_buf,
@@ -91,6 +93,8 @@
     tile_loads = [
         pltpu.make_async_copy(w_hbm, w_ref, load_sem.at[1]),
         pltpu.make_async_copy(col_hbm, col_ref, load_sem.at[2]),
+        pltpu.make_async_copy(owner_hbm, owner_ref, load_sem.at[3]),
+        pltpu.make_async_copy(block_hbm, block_ref, load_sem.at[4]),
     ]
     for tile_load in tile_loads:
         tile_load.start()
@@ -152,15 +156,12 @@
     for p in range(slices):
         part[p] = local[:, p * LANES : (p + 1) * LANES].astype(BF16)
 
-    for tile_load in tile_loads:
-        tile_load.wait()
     pl.semaphore_wait(barrier, slices - 1 + outer - 1)
 
     copies = []
     for d in range(1, slices):
         peer = flip(slot, d)
         copies.append(send(part.at[peer], rs_buf.at[d], rs_sems, (d,), member(peer)))
-    lax.fori_loop(cuts[0], cuts[1], build, 0)
     total = part[slot].astype(F32)
     for d in range(1, slices):
         copies[d - 1].wait_recv()
@@ -171,6 +172,8 @@
     copies = []
     for d in range(1, outer):
         copies.append(send(z_send, z_buf.at[d], z_sems, (d,), across(flip(group, d))))
+    for tile_load in tile_loads:
+        tile_load.wait()
     lax.fori_loop(cuts[1], cuts[2], build, 0)
     total = total + uq[slot]
     for d in range(1, outer):
@@ -207,7 +210,7 @@
         done = []
 
         def push(f, m, piece, sems, at, device):
-            source = buf.at[place(f, m, core_at), piece]
+            source = buf.at[place(f, m, core_at)]
             copy = send(source, source, sems, (which, piece) + at, (region, device))
             done.append(copy)
             return copy
@@ -226,8 +229,8 @@
             f, m = flip(far_at, fd), flip(mid_at, md)
             core_copies.append(push(f, m, piece, core_sems, (md, fd), partner))
 
-        order = [1] + list(range(far - 1, 1, -1)) if far > 1 else []
-        steps = [(fd, piece) for fd in order for piece in range(blocks_dev)]
+        order = list(range(1, far))
+        steps = [(fd, piece) for fd in order for piece in range(1)]
         far_copies = {
             (fd, piece): push(
                 far_at, mid_at, piece, far_sems, (fd,), place(flip(far_at, fd), mid_at, core_at)
@@ -235,9 +238,9 @@
             for fd, piece in steps
         }
         queue = []
-        for piece in range(blocks_dev):
+        for piece in range(1):
             queue.append((0, piece, to_mids(0, piece)))
-        for piece in range(blocks_dev):
+        for piece in range(1):
             to_core(0, 0, piece)
         if meanwhile is not None:
             meanwhile()
@@ -296,7 +299,6 @@
     rows_dev = database.shape[0]
     blocks_dev, tile_count, edge_count, block_rows = tile_weights.shape
     vmem = pl.BlockSpec(memory_space=pltpu.VMEM)
-    smem = pl.BlockSpec(memory_space=pltpu.SMEM)
     anywhere = pl.BlockSpec(memory_space=pl.ANY)
     dma = pltpu.SemaphoreType.DMA
     state = (plan.shards, blocks_dev, query_count, block_rows)
@@ -304,12 +306,14 @@
     return pl.pallas_call(
         functools.partial(kernel, plan),
         out_shape=jax.ShapeDtypeStruct((query_count, rows_dev), F32),
-        in_specs=[vmem, anywhere, vmem, anywhere, anywhere, smem, smem],
+        in_specs=[vmem, anywhere, vmem, anywhere, anywhere, anywhere, anywhere],
         out_specs=vmem,
         scratch_shapes=[
             pltpu.VMEM((rows_dev, width), BF16),
             pltpu.VMEM(tile_weights.shape, BF16),
             pltpu.VMEM(tile_columns.shape, jnp.int32),
+            pltpu.SMEM(tile_owner.shape, jnp.int32),
+            pltpu.SMEM(tile_block.shape, jnp.int32),
             pltpu.VMEM((plan.slices,) + piece, F32),
             pltpu.VMEM((plan.slices,) + piece, BF16),
             pltpu.VMEM((plan.slices,) + piece, BF16),
@@ -320,13 +324,13 @@
             pltpu.VMEM((blocks_dev, query_count, block_rows), F32),
             pltpu.VMEM(state, BF16),
             pltpu.VMEM(state, BF16),
-            dma((3,)),
+            dma((5,)),
             dma((2, plan.slices)),
             dma((2, plan.outer)),
             dma((2, plan.slices)),
-            dma((2, 2, blocks_dev, plan.far)),
-            dma((2, 2, blocks_dev, plan.mid, plan.far)),
-            dma((2, 2, blocks_dev, plan.mid, plan.far)),
+            dma((2, 2, 1, plan.far)),
+            dma((2, 2, 1, plan.mid, plan.far)),
+            dma((2, 2, 1, plan.mid, plan.far)),
         ],
         compiler_params=pltpu.CompilerParams(collective_id=0, has_side_effects=True),
         name="expand_and_diffuse",

time: 42.2 us -> 41.9 us (level)
  Pallas kernels: 40.5 us -> 39.9 us
    pallas_call x1, Pallas kernels: 40.5 us -> 39.9 us  [per_device(): pl.pallas_call(functools.partial(kernel, plan), out_shape=jax.ShapeDtypeS...]
where the time goes in v3:
time: 41.9 us; the launch traced here: 41.4 us
  Pallas kernels  39.9 us (95%)
  local copies, waits for them, and re-layouts  1.54 us (4%)
    pallas_call x1, Pallas kernels, per_device(): pl.pallas_call(functools.partial(kernel, plan), out_shape=jax.ShapeDtypeS...  39.9 us
    unnamed x1, local copies, waits for them, and re-layouts  1.54 us

profile of v3, /device:TPU:0, one launch (start us, length us, event | category | flops | bytes accessed | tf_op | source)
XLA Modules:
  0.0 41.4 jit_solution(4086528282119622859)
XLA Ops:
  0.0 39.9 %expand_and_diffuse.1 = f32[48,512]{1,0:T(8,128)} custom-call(bf16[48,1024]{1,0:T(8,128)(2,1)} %q_ref.1, bf16[512,1024]{1,0:T(8,128)(2,1)} %db_hbm.1, s32[10,48]{1,0:T(8,128)} %bitcast.1, bf16[2,13,4,256]{3,2,1,0:T(4,128)(2,1)} %w_hbm.1, s32[2,13,4,256]{3,2,1,0:T(4,128)} %col_hbm.1, s32[2,13]{1,0:T(2,128)} %owner_hbm.1, s32[2,13]{1,0:T(2,128)} %block_hbm.1), custom_call_target="tpu_custom_call" | custom-call | tf_op jit(solution)/shard_map/expand_and_diffuse/pallas_call | solution.py:306
  39.9 1.5 %copy.9 = f32[48,512]{1,0:T(8,128)} copy(f32[48,512]{1,0:T(8,128)} %expand_and_diffuse.1) | data formatting | bytes 196608
